TPU v7x, 32 devices: a whole 2x2x4 slice. The times are simulated.
32 devices in a mesh: snap: 2 (over x), row: 16 (over z, y, core).
Axes of the slice: x: 2, y: 2, z: 4, core: 2. Of those that a mesh axis runs over, the one named last changes fastest.
Arguments:
- snapshots: bfloat16 [256, 262144], P('snap', 'row'), may hold values from -64 to 64
- counts: int32 [16], P('row'), may hold values from 1 to 16384, 196608 in all
Outputs:
- basis: bfloat16 [256, 262144], P('snap', 'row')
- r_factor: float32 [256, 256], replicated
Inputs may be any that keep to these rules, and one draw needn't show every extreme that they name: `counts`: at least one row and at most 16384 rows are live on each index of row, and some index has all 16384 live.
All inputs are finite; a program needn't handle non-finite values. No bound on the sum of `counts` on one device may be relied on, other than what follows from the above.
Results may differ from a plain program's by a relative error of at most 0.0049.
Values may be sent and summed in bfloat16 or wider, within the bound.
A program may use at most 64 MiB of HBM per device.

v0:
```python
import functools
import math

import jax
import jax.numpy as jnp
from jax import lax
from jax.experimental import pallas as pl
from jax.experimental.pallas import tpu as pltpu
from jax.sharding import PartitionSpec as P

MESH = pl.DeviceIdType.MESH
HIGH = lax.Precision.HIGHEST
LANES = 128
SUBLANES = 8


def gram_of(block):
    return lax.dot_general(
        block, block, (((1,), (1,)), ((), ())), preferred_element_type=jnp.float32
    )


def factors(gram, scale):
    lower = jnp.linalg.cholesky(gram)
    r_factor = lower.T / scale
    width = gram.shape[0]
    inverse = lax.linalg.triangular_solve(
        lower, jnp.eye(width, dtype=jnp.float32), left_side=True, lower=True
    ).T
    weights = (inverse * scale).astype(jnp.bfloat16)
    return (r_factor, weights)


def apply_weights(weights, block):
    return lax.dot_general(
        weights, block, (((0,), (0,)), ((), ())), preferred_element_type=jnp.float32
    ).astype(jnp.bfloat16)


def shards(snapshots, counts):
    narrow, slots = snapshots.shape
    slot = lax.broadcasted_iota(jnp.int32, (1, slots), 1)
    live = jnp.where(slot < counts[0], snapshots, jnp.zeros_like(snapshots))
    scale = math.sqrt(slots * lax.axis_size("row"))
    whole = lax.all_gather(live, "snap", axis=0, tiled=True)
    gram = lax.psum(gram_of(whole), "row")
    r_factor, weights = factors(gram, scale)
    start = lax.axis_index("snap") * narrow
    own_weights = lax.dynamic_slice_in_dim(weights, start, narrow, 1)
    basis = apply_weights(own_weights, whole)
    return (basis, r_factor)


def mxu_nt(a, b):
    return lax.dot_general(
        a, b, (((1,), (1,)), ((), ())), preferred_element_type=jnp.float32
    )


def partial_kernel(
    pieces, counts_ref, x_ref, part_ref, first_ref, later_ref, last_ref,
    own, got, mine, near, summed, theirs,
    load_sem, send_sem, recv_sem, keep_sem, back_sem, sum_send, sum_recv, near_send, near_recv,
):
    snap = lax.axis_index("snap")
    core = lax.rem(lax.axis_index("row"), 2)
    other = {"snap": 1 - snap}
    pair = {"row": lax.axis_index("row") + 1 - 2 * core}
    narrow, slots = x_ref.shape
    half = slots // 2
    step = half // pieces
    count = counts_ref[0]

    barrier = pltpu.get_barrier_semaphore()
    pl.semaphore_signal(barrier, inc=1, device_id=other, device_id_type=MESH)
    pl.semaphore_signal(barrier, inc=1, device_id=pair, device_id_type=MESH)

    loads = []
    for c in range(2 * pieces):
        at = pl.ds(c * step, step)
        copy = pltpu.make_async_copy(x_ref.at[:, at], own.at[:, at], load_sem.at[c])
        copy.start()
        loads.append(copy)

    pl.semaphore_wait(barrier, 2)

    def send(i, src, into, dst, size):
        copy = pltpu.make_async_remote_copy(
            src_ref=x_ref.at[:, pl.ds(src, size)],
            dst_ref=into.at[:, pl.ds(dst, size)],
            send_sem=send_sem.at[i],
            recv_sem=recv_sem.at[i],
            device_id=other,
            device_id_type=MESH,
        )
        copy.start()
        return copy

    sends = [
        send(c, pl.multiple_of(snap * half + c * step, step), got, c * step, step)
        for c in range(pieces)
    ]

    def masked(block, start):
        lane = lax.broadcasted_iota(jnp.int32, block.shape, 1) + start
        return jnp.where(lane < count, block, jnp.zeros_like(block))

    total = jnp.zeros((narrow, narrow), jnp.float32)
    for c in range(2 * pieces):
        loads[c].wait()
        block = own[:, c * step:(c + 1) * step]
        total = total + mxu_nt(masked(block, c * step), block)
    mine[0] = total
    keeps = []
    start = first_ref.shape[1]
    for i, ref in enumerate((later_ref, last_ref)):
        size = ref.shape[1]
        keep = pltpu.make_async_copy(own.at[:, pl.ds(start, size)], ref, keep_sem.at[i])
        keep.start()
        keeps.append(keep)
        start += size

    rows = narrow // 2

    def sum_copy(i):
        away = pltpu.make_async_remote_copy(
            src_ref=mine.at[i, pl.ds(pl.multiple_of((1 - core) * rows, SUBLANES), rows)],
            dst_ref=near.at[i],
            send_sem=near_send.at[i],
            recv_sem=near_recv.at[i],
            device_id=pair,
            device_id_type=MESH,
        )
        away.start()
        away.wait()
        kept = mine[i, pl.ds(pl.multiple_of(core * rows, SUBLANES), rows), :]
        summed[i] = kept + near[i]
        return pltpu.make_async_remote_copy(
            src_ref=summed.at[i],
            dst_ref=theirs.at[i],
            send_sem=sum_send.at[i],
            recv_sem=sum_recv.at[i],
            device_id=other,
            device_id_type=MESH,
        )

    diagonal = sum_copy(0)
    diagonal.start()
    spare = first_ref.shape[1] - half
    ahead = spare * 3 // 4
    extras = [send(pieces, half, first_ref, half, ahead)]

    cross = jnp.zeros((narrow, narrow), jnp.float32)
    backs = []
    base = (1 - snap) * half
    for c in range(pieces):
        sends[c].wait_recv()
        here = pl.ds(c * step, step)
        back = pltpu.make_async_copy(got.at[:, here], first_ref.at[:, here], back_sem.at[c])
        back.start()
        backs.append(back)
        start = pl.multiple_of(base + c * step, step)
        block = masked(own[:, pl.ds(start, step)], start)
        cross = cross + mxu_nt(block, got[:, c * step:(c + 1) * step])
    mine[1] = jnp.where(snap == 0, cross, cross.T)
    crossed = sum_copy(1)
    crossed.start()
    at = half + ahead
    extras.append(send(pieces + 1, at, first_ref, at, spare - ahead))
    for copy in sends:
        copy.wait_send()
    for copy in keeps:
        copy.wait()
    diagonal.wait()
    part_ref[0:rows, :] = jnp.where(snap == 0, summed[0], theirs[0])
    part_ref[rows:2 * rows, :] = jnp.where(snap == 0, theirs[0], summed[0])
    crossed.wait()
    part_ref[2 * rows:3 * rows, :] = summed[1] + theirs[1]
    for copy in extras:
        copy.wait()
    for copy in backs:
        copy.wait()


def partial_grams(snapshots, counts, pieces=8):
    narrow, slots = snapshots.shape
    half = slots // 2
    step = half // pieces
    early = half + step
    last = step
    later = slots - early - last
    any_space = pl.BlockSpec(memory_space=pl.ANY)
    return pl.pallas_call(
        functools.partial(partial_kernel, pieces),
        name="partial_grams",
        out_shape=(
            jax.ShapeDtypeStruct((3 * narrow // 2, narrow), jnp.float32),
            jax.ShapeDtypeStruct((narrow, early), snapshots.dtype),
            jax.ShapeDtypeStruct((narrow, later), snapshots.dtype),
            jax.ShapeDtypeStruct((narrow, last), snapshots.dtype),
        ),
        in_specs=[
            pl.BlockSpec(memory_space=pltpu.SMEM),
            pl.BlockSpec(memory_space=pltpu.HBM),
        ],
        out_specs=(pl.BlockSpec(memory_space=pltpu.VMEM), any_space, any_space, any_space),
        scratch_shapes=[
            pltpu.VMEM((narrow, slots), snapshots.dtype),
            pltpu.VMEM((narrow, half), snapshots.dtype),
            pltpu.VMEM((2, narrow, narrow), jnp.float32),
            pltpu.VMEM((2, narrow // 2, narrow), jnp.float32),
            pltpu.VMEM((2, narrow // 2, narrow), jnp.float32),
            pltpu.VMEM((2, narrow // 2, narrow), jnp.float32),
            pltpu.SemaphoreType.DMA((2 * pieces,)),
            pltpu.SemaphoreType.DMA((pieces + 2,)),
            pltpu.SemaphoreType.DMA((pieces + 2,)),
            pltpu.SemaphoreType.DMA((2,)),
            pltpu.SemaphoreType.DMA((pieces,)),
            pltpu.SemaphoreType.DMA((2,)),
            pltpu.SemaphoreType.DMA((2,)),
            pltpu.SemaphoreType.DMA((2,)),
            pltpu.SemaphoreType.DMA((2,)),
        ],
        compiler_params=pltpu.CompilerParams(
            collective_id=0, has_side_effects=True, vmem_limit_bytes=62 << 20
        ),
    )(counts, snapshots)


def reduce_kernel(n, part_ref, out_ref, parts, send_sem, recv_sem, out_send, out_recv):
    me = lax.axis_index("row")
    core, chip = lax.rem(me, 2), lax.div(me, 2)
    chips = n // 2
    rows = part_ref.shape[0] // chips
    barrier = pltpu.get_barrier_semaphore()
    for d in range(1, n):
        peer = lax.rem(me + d, n)
        pl.semaphore_signal(barrier, inc=1, device_id={"row": peer}, device_id_type=MESH)
    pl.semaphore_wait(barrier, n - 1)

    def at(i):
        return pl.ds(pl.multiple_of(i * rows, SUBLANES), rows)

    copies = []
    for d in range(1, chips):
        peer = lax.rem(chip + d, chips)
        copy = pltpu.make_async_remote_copy(
            src_ref=part_ref.at[at(peer)],
            dst_ref=parts.at[d - 1],
            send_sem=send_sem.at[d - 1],
            recv_sem=recv_sem.at[d - 1],
            device_id={"row": 2 * peer + core},
            device_id_type=MESH,
        )
        copy.start()
        copies.append(copy)
    total = part_ref[at(chip), :]
    for d in range(1, chips):
        copies[d - 1].wait_recv()
        total = total + parts[d - 1]
    out_ref[core, at(chip), :] = total
    results = []
    for d in range(1, n):
        peer = lax.rem(me + d, n)
        copy = pltpu.make_async_remote_copy(
            src_ref=out_ref.at[core, at(chip)],
            dst_ref=out_ref.at[core, at(chip)],
            send_sem=out_send.at[d - 1],
            recv_sem=out_recv.at[d - 1],
            device_id={"row": peer},
            device_id_type=MESH,
        )
        copy.start()
        results.append(copy)
    for copy in copies:
        copy.wait_send()
    for copy in results:
        copy.wait()


def reduce_rows(part):
    n = lax.axis_size("row")
    chips = n // 2
    rows = part.shape[0] // chips
    vmem = pl.BlockSpec(memory_space=pltpu.VMEM)
    return pl.pallas_call(
        functools.partial(reduce_kernel, n),
        name="reduce_rows",
        out_shape=jax.ShapeDtypeStruct((2, *part.shape), part.dtype),
        in_specs=[vmem],
        out_specs=vmem,
        scratch_shapes=[
            pltpu.VMEM((chips - 1, rows, part.shape[1]), part.dtype),
            pltpu.SemaphoreType.DMA((chips - 1,)),
            pltpu.SemaphoreType.DMA((chips - 1,)),
            pltpu.SemaphoreType.DMA((n - 1,)),
            pltpu.SemaphoreType.DMA((n - 1,)),
        ],
        compiler_params=pltpu.CompilerParams(
            collective_id=1, has_side_effects=True, vmem_limit_bytes=8 << 20
        ),
        cost_estimate=pl.CostEstimate(
            flops=1 << 30, bytes_accessed=48 << 20, transcendentals=0
        ),
    )(part)


def eliminate(groups):
    shape = groups[0].shape
    tall = shape[0]
    lane = lax.broadcasted_iota(jnp.int32, shape, 1)
    sub = lax.broadcasted_iota(jnp.int32, shape, 0)
    groups = list(groups)
    count = len(groups)

    def line(block, p):
        return jnp.broadcast_to(block[p:p + 1, :], shape)

    for g in range(count):
        columns = [
            [
                jnp.broadcast_to(groups[v][:, g * tall + q:g * tall + q + 1], shape)
                for v in range(g, count)
            ]
            for q in range(tall)
        ]
        for p in range(tall):
            here = lane == g * tall + p
            pivot = line(columns[p][0], p)
            root = lax.rsqrt(pivot)
            root = root * (1.5 - 0.5 * pivot * root * root)
            lefts = [column * root for column in columns[p]]
            lefts[0] = jnp.where(sub > p, lefts[0], 0.0)
            for q in range(p + 1, tall):
                top = line(columns[q][0], p) * root
                columns[q] = [c - m * top for c, m in zip(columns[q], lefts)]
            row = jnp.where(here, root, line(groups[g], p) * root)
            for v in range(g, count):
                old = groups[v]
                new = jnp.where(here, 0.0, old) - lefts[v - g] * row
                if v == g:
                    new = jnp.where(sub == p, row, jnp.where(sub > p, new, old))
                groups[v] = new
    return groups


def factor_kernel(scale, gram_ref, r_ref, own_ref, other_ref, work, roots):
    narrow = gram_ref.shape[2]
    rows = narrow // 2
    snap = lax.axis_index("snap")
    row = lax.broadcasted_iota(jnp.int32, (narrow, narrow), 0)
    col = lax.broadcasted_iota(jnp.int32, (narrow, narrow), 1)

    def gram(i):
        here = slice(i * rows, (i + 1) * rows)
        return jnp.concatenate([gram_ref[0, here, :], gram_ref[1, here, :]], axis=0)

    def dot(a, b, dims):
        return lax.dot_general(
            a, b, (dims, ((), ())), precision=HIGH, preferred_element_type=jnp.float32
        )

    def diagonal(which):
        full = work[which]
        inverse = jnp.where(col <= row, full, 0.0)
        upper = jnp.where(col > row, full, 0.0)
        upper = jnp.where(col == row, 1.0 / full, upper)
        return inverse, upper

    work[0] = gram(0)
    work[1] = gram(1)

    @pl.loop(0, 2)
    def _(block):
        groups = [
            work[block, SUBLANES * v:SUBLANES * (v + 1), :] for v in range(narrow // SUBLANES)
        ]
        for v, group in enumerate(eliminate(groups)):
            work[block, SUBLANES * v:SUBLANES * (v + 1), :] = group

        @pl.when(block == 0)
        def _():
            inverse, _ = diagonal(0)
            right = dot(inverse, gram(2), ((1,), (0,)))
            roots[...] = right
            work[1] = work[1] - dot(right, right, ((0,), (0,)))

    inverse0, upper0 = diagonal(0)
    inverse1, upper1 = diagonal(1)
    right = roots[...]
    below = -dot(inverse1, dot(right, inverse0, ((0,), (0,))), ((1,), (0,)))
    r_ref[0:narrow, 0:narrow] = upper0 / scale
    r_ref[0:narrow, narrow:] = right / scale
    r_ref[narrow:, 0:narrow] = jnp.zeros_like(right)
    r_ref[narrow:, narrow:] = upper1 / scale
    own = jnp.where(snap == 0, inverse0, inverse1)
    own_ref[...] = (own * scale).astype(own_ref.dtype)
    other = jnp.where(snap == 0, 0.0, below)
    other_ref[...] = (other * scale).astype(other_ref.dtype)


def factor(gram, scale, dtype):
    narrow = gram.shape[2]
    vmem = pl.BlockSpec(memory_space=pltpu.VMEM)
    return pl.pallas_call(
        functools.partial(factor_kernel, scale),
        name="factor",
        out_shape=(
            jax.ShapeDtypeStruct((2 * narrow, 2 * narrow), jnp.float32),
            jax.ShapeDtypeStruct((narrow, narrow), dtype),
            jax.ShapeDtypeStruct((narrow, narrow), dtype),
        ),
        in_specs=[vmem],
        out_specs=(vmem, vmem, vmem),
        scratch_shapes=[
            pltpu.VMEM((2, narrow, narrow), jnp.float32),
            pltpu.VMEM((narrow, narrow), jnp.float32),
        ],
        compiler_params=pltpu.CompilerParams(vmem_limit_bytes=8 << 20),
        cost_estimate=pl.CostEstimate(
            flops=1 << 30, bytes_accessed=96 << 20, transcendentals=0
        ),
    )(gram)


def basis_kernel(
    pieces, first_piece, counts_ref, own_w, other_w, own_ref, got_ref, *rest
):
    out_ref, stage, sems = rest[-3:]
    narrow, width = got_ref.shape
    step = width // pieces
    count = counts_ref[0]
    weights = jnp.concatenate([own_w[...], other_w[...]], axis=1)
    copies = []
    for c in range(pieces):
        here = pl.ds(c * step, step)
        start = first_piece + c * step
        both = jnp.concatenate(
            [own_ref[:, start:start + step], got_ref[:, c * step:(c + 1) * step]], axis=0
        )
        value = lax.dot_general(
            weights, both, (((1,), (0,)), ((), ())), preferred_element_type=jnp.float32
        )
        lane = lax.broadcasted_iota(jnp.int32, value.shape, 1) + start
        stage[:, c * step:(c + 1) * step] = jnp.where(lane < count, value, 0.0).astype(stage.dtype)
        copy = pltpu.make_async_copy(
            stage.at[:, here], out_ref.at[:, pl.ds(start, step)], sems.at[c]
        )
        copy.start()
        copies.append(copy)
    for copy in copies:
        copy.wait()


def form_basis(counts, own_w, other_w, snapshots, got, start, before=None, most=2048):
    narrow, width = got.shape
    pieces = next(n for n in range(1, width) if width % (n * LANES) == 0 and width // n <= most)
    vmem = pl.BlockSpec(memory_space=pltpu.VMEM)
    hbm = pl.BlockSpec(memory_space=pltpu.HBM)
    operands = [counts, own_w, other_w, snapshots, got]
    specs = [pl.BlockSpec(memory_space=pltpu.SMEM), vmem, vmem, vmem, vmem]
    aliases = {}
    if before is not None:
        aliases = {len(operands): 0}
        operands.append(before)
        specs.append(hbm)
    return pl.pallas_call(
        functools.partial(basis_kernel, pieces, start),
        name="form_basis",
        out_shape=jax.ShapeDtypeStruct(snapshots.shape, snapshots.dtype),
        in_specs=specs,
        out_specs=hbm,
        input_output_aliases=aliases,
        scratch_shapes=[
            pltpu.VMEM((narrow, width), snapshots.dtype),
            pltpu.SemaphoreType.DMA((pieces,)),
        ],
        compiler_params=pltpu.CompilerParams(vmem_limit_bytes=16 << 20),
        cost_estimate=pl.CostEstimate(
            flops=4 * narrow * narrow * width,
            bytes_accessed=8 * narrow * width,
            transcendentals=0,
        ),
    )(*operands)


def halves(snapshots, counts):
    slots = snapshots.shape[1]
    scale = math.sqrt(slots * lax.axis_size("row"))
    part, *got = partial_grams(snapshots, counts)
    got[1:] = [lax.ppermute(piece, "snap", [(0, 1)]) for piece in got[1:]]
    gram = reduce_rows(part)
    r_factor, own_w, other_w = factor(gram, scale, snapshots.dtype)
    basis, start = None, 0
    for piece in got:
        basis = form_basis(counts, own_w, other_w, snapshots, piece, start, basis)
        start += piece.shape[1]
    return (basis, r_factor)


def two_halves(mesh):
    return mesh.shape["snap"] == 2 and mesh.shape["row"] == 16


def solution(mesh):
    placed = (P("snap", "row"), P("row"))
    body = halves if two_halves(mesh) else shards
    return jax.shard_map(
        body, mesh=mesh, in_specs=placed, out_specs=(P("snap", "row"), P()), check_vma=False
    )
```

profile of v0, /device:TPU:31, one launch (start us, length us, event | category | flops | bytes accessed | tf_op | source)
XLA Modules:
  0.0 100.3 jit_solution(7937529208775337382)
XLA Ops:
  1.3 55.2 %partial_grams.1 = (f32[192,128]{1,0:T(8,128)}, bf16[128,9216]{1,0:T(8,128)(2,1)}, bf16[128,6144]{1,0:T(8,128)(2,1)}, bf16[128,1024]{1,0:T(8,128)(2,1)}) custom-call(s32[1]{0:T(128)S(6)} %copy.8.counts_ref, bf16[128,16384]{1,0:T(8,128)(2,1)} %own_ref.5), custom_call_target="tpu_custom_call" | custom-call | tf_op jit(solution)/shard_map/partial_grams/pallas_call | solution.py:193
  56.5 0.0 copy-start
  56.5 0.0 copy-start.1
  56.5 1.6 %collective-permute-start.1 = (bf16[128,6144]{1,0:T(8,128)(2,1)}, bf16[128,6144]{1,0:T(8,128)(2,1)S(1)}, u32[]{:S(2)}, u32[]{:S(2)}) collective-permute-start(bf16[128,6144]{1,0:T(8,128)(2,1)} %get-tuple-element.13), channel_id=1, source_target_pairs={{0,16},{1,17},{2,18},{3,19},{4,20},{5,21},{6,22},{7,23},{8,24},{9,... | collective-permute-start | bytes 4718600 | tf_op jit(solution)/shard_map/ppermute | solution.py:491
  58.1 1.4 %collective-permute-start = (bf16[128,1024]{1,0:T(8,128)(2,1)}, bf16[128,1024]{1,0:T(8,128)(2,1)S(1)}, u32[]{:S(2)}, u32[]{:S(2)}) collective-permute-start(bf16[128,1024]{1,0:T(8,128)(2,1)} %get-tuple-element.12), channel_id=1, source_target_pairs={{0,16},{1,17},{2,18},{3,19},{4,20},{5,21},{6,22},{7,23},{8,24},{9,... | collective-permute-start | bytes 786440 | tf_op jit(solution)/shard_map/ppermute | solution.py:491
  59.5 0.0 copy-start.2
  59.5 0.9 copy-done.2
  60.4 13.8 %reduce_rows.1.gram_ref = f32[2,192,128]{2,1,0:T(8,128)S(1)} custom-call(f32[192,128]{1,0:T(8,128)S(1)} %copy-done.2), custom_call_target="tpu_custom_call" | custom-call | flops 1073741824 | bytes 50331648 | tf_op jit(solution)/shard_map/reduce_rows/pallas_call | solution.py:286
  74.2 12.6 %factor.1 = (f32[256,256]{1,0:T(8,128)}, bf16[128,128]{1,0:T(8,128)(2,1)S(1)}, bf16[128,128]{1,0:T(8,128)(2,1)S(1)}) custom-call(f32[2,192,128]{2,1,0:T(8,128)S(1)} %reduce_rows.1.gram_ref), custom_call_target="tpu_custom_call" | custom-call | flops 1073741824 | bytes 100663296 | tf_op jit(solution)/shard_map/factor/pallas_call | solution.py:405
  86.8 0.0 copy-done
  86.8 0.0 copy-done.1
  86.8 1.7 %form_basis.3.rest_0_ = bf16[128,16384]{1,0:T(8,128)(2,1)} custom-call(s32[1]{0:T(128)S(6)} %copy.8.counts_ref, bf16[128,128]{1,0:T(8,128)(2,1)S(1)} %get-tuple-element.10.own_w, bf16[128,128]{1,0:T(8,128)(2,1)S(1)} %get-tuple-element.11.other_w, bf16[128,16384]{1,0:T(8,128)(2,1)S(1)} %copy-done, bf16[128,9216]{1,0:T(8,128)(2,1)S(1)} %copy-done.1), custom_call_target="tpu_custom_call" | custom-call | flops 603979776 | bytes 9437184 | tf_op jit(solution)/shard_map/form_basis/pallas_call | solution.py:467
  88.5 5.2 %collective-permute-done.1.got_ref = bf16[128,6144]{1,0:T(8,128)(2,1)S(1)} collective-permute-done((bf16[128,6144]{1,0:T(8,128)(2,1)}, bf16[128,6144]{1,0:T(8,128)(2,1)S(1)}, u32[]{:S(2)}, u32[]{:S(2)}) %collective-permute-start.1) | collective-permute-done | bytes 1572896 | tf_op jit(solution)/shard_map/ppermute | solution.py:491
  93.7 1.5 %form_basis.4.rest_0_ = bf16[128,16384]{1,0:T(8,128)(2,1)} custom-call(s32[1]{0:T(128)S(6)} %copy.8.counts_ref, bf16[128,128]{1,0:T(8,128)(2,1)S(1)} %get-tuple-element.10.own_w, bf16[128,128]{1,0:T(8,128)(2,1)S(1)} %get-tuple-element.11.other_w, bf16[128,16384]{1,0:T(8,128)(2,1)S(1)} %copy-done, ...), custom_call_target="tpu_custom_call", output_to_operand_aliasing={{}: (5, {})} | custom-call | flops 402653184 | bytes 6291456 | tf_op jit(solution)/shard_map/form_basis/pallas_call | solution.py:467
  95.2 4.1 %collective-permute-done.got_ref = bf16[128,1024]{1,0:T(8,128)(2,1)S(1)} collective-permute-done((bf16[128,1024]{1,0:T(8,128)(2,1)}, bf16[128,1024]{1,0:T(8,128)(2,1)S(1)}, u32[]{:S(2)}, u32[]{:S(2)}) %collective-permute-start) | collective-permute-done | bytes 262176 | tf_op jit(solution)/shard_map/ppermute | solution.py:491
  99.4 0.9 form_basis.5
Async XLA Ops:
  56.5 30.3 %copy-start = (bf16[128,16384]{1,0:T(8,128)(2,1)S(1)}, bf16[128,16384]{1,0:T(8,128)(2,1)}, u32[]{:S(2)}) copy-start(bf16[128,16384]{1,0:T(8,128)(2,1)} %own_ref.5) | copy-start | bytes 12582916
  56.5 30.3 %copy-start.1 = (bf16[128,9216]{1,0:T(8,128)(2,1)S(1)}, bf16[128,9216]{1,0:T(8,128)(2,1)}, u32[]{:S(2)}) copy-start(bf16[128,9216]{1,0:T(8,128)(2,1)} %get-tuple-element.14.got_ref) | copy-start | bytes 7077892
  56.5 37.2 %collective-permute-start.1 = (bf16[128,6144]{1,0:T(8,128)(2,1)}, bf16[128,6144]{1,0:T(8,128)(2,1)S(1)}, u32[]{:S(2)}, u32[]{:S(2)}) collective-permute-start(bf16[128,6144]{1,0:T(8,128)(2,1)} %get-tuple-element.13), channel_id=1, source_target_pairs={{0,16},{1,17},{2,18},{3,19},{4,20},{5,21},{6,22},{7,23},{8,24},{9,... | collective-permute-start | bytes 4718600 | tf_op jit(solution)/shard_map/ppermute | solution.py:491
  58.1 41.3 %collective-permute-start = (bf16[128,1024]{1,0:T(8,128)(2,1)}, bf16[128,1024]{1,0:T(8,128)(2,1)S(1)}, u32[]{:S(2)}, u32[]{:S(2)}) collective-permute-start(bf16[128,1024]{1,0:T(8,128)(2,1)} %get-tuple-element.12), channel_id=1, source_target_pairs={{0,16},{1,17},{2,18},{3,19},{4,20},{5,21},{6,22},{7,23},{8,24},{9,... | collective-permute-start | bytes 786440 | tf_op jit(solution)/shard_map/ppermute | solution.py:491
  59.5 0.9 copy-start.2
where the time goes:
time: 102 us; the launch traced here: 100 us
  Pallas kernels  85.7 us (84%)
  waiting for transfers between devices  9.35 us (9%)
  starting transfers between devices  2.98 us (3%)
  between operations  1.35 us (1%)
    pallas_call x1, Pallas kernels, partial_grams(): pl.pallas_call(functools.partial(partial_kernel, pieces), name='partial_g...  55.2 us
    pallas_call x1, Pallas kernels, reduce_rows(): pl.pallas_call(functools.partial(reduce_kernel, n), name='reduce_rows', o...  13.8 us
    pallas_call x1, Pallas kernels, factor(): pl.pallas_call(functools.partial(factor_kernel, scale), name='factor', ou...  12.6 us
    ppermute x2, waiting for transfers between devices, halves(): got[1:] = [lax.ppermute(piece, 'snap', [(0, 1)]) for piece in got[1:]]  9.35 us
    pallas_call x3, Pallas kernels, form_basis(): pl.pallas_call(functools.partial(basis_kernel, pieces, start), name='form...  4.16 us
    ppermute x2, starting transfers between devices, halves(): got[1:] = [lax.ppermute(piece, 'snap', [(0, 1)]) for piece in got[1:]]  2.98 us
  transfers between devices with their start and end apart: 2, of which 2 were waited for; matrix products, arithmetic and copies ran while one was open for 0% of the time, Pallas kernels for 30%

commit v1 on v0

v1 whole, which is shorter than its diff:
```python
import functools
import math

import jax
import jax.numpy as jnp
from jax import lax
from jax.experimental import pallas as pl
from jax.experimental.pallas import tpu as pltpu
from jax.sharding import PartitionSpec as P

MESH = pl.DeviceIdType.MESH
HIGH = lax.Precision.HIGHEST
LANES = 128
SUBLANES = 8


def gram_of(block):
    return lax.dot_general(
        block, block, (((1,), (1,)), ((), ())), preferred_element_type=jnp.float32
    )


def factors(gram, scale):
    lower = jnp.linalg.cholesky(gram)
    r_factor = lower.T / scale
    width = gram.shape[0]
    inverse = lax.linalg.triangular_solve(
        lower, jnp.eye(width, dtype=jnp.float32), left_side=True, lower=True
    ).T
    weights = (inverse * scale).astype(jnp.bfloat16)
    return (r_factor, weights)


def apply_weights(weights, block):
    return lax.dot_general(
        weights, block, (((0,), (0,)), ((), ())), preferred_element_type=jnp.float32
    ).astype(jnp.bfloat16)


def shards(snapshots, counts):
    narrow, slots = snapshots.shape
    slot = lax.broadcasted_iota(jnp.int32, (1, slots), 1)
    live = jnp.where(slot < counts[0], snapshots, jnp.zeros_like(snapshots))
    scale = math.sqrt(slots * lax.axis_size("row"))
    whole = lax.all_gather(live, "snap", axis=0, tiled=True)
    gram = lax.psum(gram_of(whole), "row")
    r_factor, weights = factors(gram, scale)
    start = lax.axis_index("snap") * narrow
    own_weights = lax.dynamic_slice_in_dim(weights, start, narrow, 1)
    basis = apply_weights(own_weights, whole)
    return (basis, r_factor)


def mxu_nt(a, b):
    return lax.dot_general(
        a, b, (((1,), (1,)), ((), ())), preferred_element_type=jnp.float32
    )


def eliminate(groups):
    shape = groups[0].shape
    tall = shape[0]
    lane = lax.broadcasted_iota(jnp.int32, shape, 1)
    sub = lax.broadcasted_iota(jnp.int32, shape, 0)
    groups = list(groups)
    count = len(groups)

    def line(block, p):
        return jnp.broadcast_to(block[p:p + 1, :], shape)

    for g in range(count):
        columns = [
            [
                jnp.broadcast_to(groups[v][:, g * tall + q:g * tall + q + 1], shape)
                for v in range(g, count)
            ]
            for q in range(tall)
        ]
        for p in range(tall):
            here = lane == g * tall + p
            pivot = line(columns[p][0], p)
            root = lax.rsqrt(pivot)
            root = root * (1.5 - 0.5 * pivot * root * root)
            lefts = [column * root for column in columns[p]]
            lefts[0] = jnp.where(sub > p, lefts[0], 0.0)
            for q in range(p + 1, tall):
                top = line(columns[q][0], p) * root
                columns[q] = [c - m * top for c, m in zip(columns[q], lefts)]
            row = jnp.where(here, root, line(groups[g], p) * root)
            for v in range(g, count):
                old = groups[v]
                new = jnp.where(here, 0.0, old) - lefts[v - g] * row
                if v == g:
                    new = jnp.where(sub == p, row, jnp.where(sub > p, new, old))
                groups[v] = new
    return groups


def factor_body(scale, gram_ref, r_ref, own_ref, other_ref, work, roots):
    narrow = gram_ref.shape[2]
    rows = narrow // 2
    snap = lax.axis_index("snap")
    row = lax.broadcasted_iota(jnp.int32, (narrow, narrow), 0)
    col = lax.broadcasted_iota(jnp.int32, (narrow, narrow), 1)

    def gram(i):
        here = slice(i * rows, (i + 1) * rows)
        return jnp.concatenate([gram_ref[0, here, :], gram_ref[1, here, :]], axis=0)

    def dot(a, b, dims):
        return lax.dot_general(
            a, b, (dims, ((), ())), precision=HIGH, preferred_element_type=jnp.float32
        )

    def diagonal(which):
        full = work[which]
        inverse = jnp.where(col <= row, full, 0.0)
        upper = jnp.where(col > row, full, 0.0)
        upper = jnp.where(col == row, 1.0 / full, upper)
        return inverse, upper

    work[0] = gram(0)
    work[1] = gram(1)

    @pl.loop(0, 2)
    def _(block):
        groups = [
            work[block, SUBLANES * v:SUBLANES * (v + 1), :] for v in range(narrow // SUBLANES)
        ]
        for v, group in enumerate(eliminate(groups)):
            work[block, SUBLANES * v:SUBLANES * (v + 1), :] = group

        @pl.when(block == 0)
        def _():
            inverse, _ = diagonal(0)
            right = dot(inverse, gram(2), ((1,), (0,)))
            roots[...] = right
            work[1] = work[1] - dot(right, right, ((0,), (0,)))

    inverse0, upper0 = diagonal(0)
    inverse1, upper1 = diagonal(1)
    right = roots[...]
    below = -dot(inverse1, dot(right, inverse0, ((0,), (0,))), ((1,), (0,)))
    r_ref[0:narrow, 0:narrow] = upper0 / scale
    r_ref[0:narrow, narrow:] = right / scale
    r_ref[narrow:, 0:narrow] = jnp.zeros_like(right)
    r_ref[narrow:, narrow:] = upper1 / scale
    own = jnp.where(snap == 0, inverse0, inverse1)
    own_ref[...] = (own * scale).astype(own_ref.dtype)
    other = jnp.where(snap == 0, 0.0, below)
    other_ref[...] = (other * scale).astype(other_ref.dtype)


def meet(sem, stage, chip_row, core):
    y, z = lax.rem(chip_row, 2), lax.div(chip_row, 2)
    last = lax.axis_size("row") // 4 - 1

    def signal(chip):
        pl.semaphore_signal(
            sem.at[stage], inc=1, device_id={"row": 2 * chip + core}, device_id_type=MESH
        )

    signal(chip_row + 1 - 2 * y)

    @pl.when(z > 0)
    def _():
        signal(chip_row - 2)

    @pl.when(z < last)
    def _():
        signal(chip_row + 2)


def meetings(chip_row):
    z = lax.div(chip_row, 2)
    last = lax.axis_size("row") // 4 - 1
    return 1 + jnp.where(z > 0, 1, 0) + jnp.where(z < last, 1, 0)


def panel_kernel(
    units, scale, counts_ref, x_ref, own, got, r_ref, own_w_ref, other_w_ref,
    mine, near, summed, theirs, part, parts, gram_ref, work, roots,
    load_sem, send_sem, recv_sem, met, near_send, near_recv, sum_send, sum_recv,
    part_send, part_recv, out_send, out_recv, pair_send, pair_recv,
):
    snap = lax.axis_index("snap")
    me = lax.axis_index("row")
    core, chip = lax.rem(me, 2), lax.div(me, 2)
    chips = lax.axis_size("row") // 2
    other = {"snap": 1 - snap}
    pair = {"row": me + 1 - 2 * core}
    narrow, slots = x_ref.shape
    step = slots // units
    halfway = units // 2
    half = slots // 2
    count = counts_ref[0]
    rows = narrow // 2
    y, z = lax.rem(chip, 2), lax.div(chip, 2)
    last = chips // 2 - 1

    barrier = pltpu.get_barrier_semaphore()

    def greet(device):
        pl.semaphore_signal(barrier, inc=1, device_id=device, device_id_type=MESH)

    greet(other)
    greet(pair)
    greet({"row": 2 * (chip + 1 - 2 * y) + core})

    @pl.when(z > 0)
    def _():
        greet({"row": me - 4})

    @pl.when(z < last)
    def _():
        greet({"row": me + 4})

    wide = 8
    span = slots // wide
    loads = []
    for c in range(wide):
        at = pl.ds(c * span, span)
        copy = pltpu.make_async_copy(x_ref.at[:, at], own.at[:, at], load_sem.at[c])
        copy.start()
        loads.append(copy)

    pl.semaphore_wait(barrier, 2 + meetings(chip))

    def bulk(u):
        at = pl.ds(u * step, step)
        return pltpu.make_async_remote_copy(
            src_ref=x_ref.at[:, at], dst_ref=got.at[:, at],
            send_sem=send_sem.at[u], recv_sem=recv_sem.at[u],
            device_id=other, device_id_type=MESH,
        )

    def send(low, high):
        @pl.when(snap == 0)
        def _():
            for u in range(low, high):
                bulk(u).start()

        top = min(high, halfway)

        @pl.when(snap == 1)
        def _():
            for u in range(low, top):
                bulk(halfway + u).start()

    send(0, 6)

    def masked(block, start):
        lane = lax.broadcasted_iota(jnp.int32, block.shape, 1) + start
        return jnp.where(lane < count, block, jnp.zeros_like(block))

    total = jnp.zeros((narrow, narrow), jnp.float32)
    for c in range(wide):
        loads[c].wait()
        block = own[:, c * span:(c + 1) * span]
        total = total + mxu_nt(masked(block, c * span), block)
    mine[0] = total

    def near_copy(i):
        return pltpu.make_async_remote_copy(
            src_ref=mine.at[i, pl.ds(pl.multiple_of((1 - core) * rows, SUBLANES), rows)],
            dst_ref=near.at[i],
            send_sem=near_send.at[i], recv_sem=near_recv.at[i],
            device_id=pair, device_id_type=MESH,
        )

    def sum_copy(i):
        away = near_copy(i)
        away.start()
        away.wait()
        kept = mine[i, pl.ds(pl.multiple_of(core * rows, SUBLANES), rows), :]
        summed[i] = kept + near[i]
        return pltpu.make_async_remote_copy(
            src_ref=summed.at[i], dst_ref=theirs.at[i],
            send_sem=sum_send.at[i], recv_sem=sum_recv.at[i],
            device_id=other, device_id_type=MESH,
        )

    diagonal = sum_copy(0)
    diagonal.start()
    send(6, halfway + 1)

    for stage in range(met.shape[0]):
        meet(met, stage, chip, core)
        pl.semaphore_wait(met.at[stage], meetings(chip))

    mine[1] = jnp.zeros((narrow, narrow), jnp.float32)
    for u in range(halfway):
        @pl.when(snap == 1)
        def _():
            bulk(u).wait_recv()
            start = u * step
            block = masked(own[:, start:start + step], start)
            mine[1] = mine[1] + mxu_nt(got[:, start:start + step], block)

        @pl.when(snap == 0)
        def _():
            bulk(halfway + u).wait_recv()
            start = half + u * step
            block = masked(own[:, start:start + step], start)
            mine[1] = mine[1] + mxu_nt(block, got[:, start:start + step])

    crossed = sum_copy(1)
    crossed.start()
    send(halfway + 1, units)

    diagonal.wait()
    part[0:rows, :] = jnp.where(snap == 0, summed[0], theirs[0])
    part[rows:2 * rows, :] = jnp.where(snap == 0, theirs[0], summed[0])
    crossed.wait()
    part[2 * rows:3 * rows, :] = summed[1] + theirs[1]

    lines = part.shape[0] // chips

    def at(i):
        return pl.ds(pl.multiple_of(i * lines, SUBLANES), lines)

    copies = []
    for d in range(1, chips):
        peer = lax.rem(chip + d, chips)
        copy = pltpu.make_async_remote_copy(
            src_ref=part.at[at(peer)], dst_ref=parts.at[d - 1],
            send_sem=part_send.at[d - 1], recv_sem=part_recv.at[d - 1],
            device_id={"row": 2 * peer + core}, device_id_type=MESH,
        )
        copy.start()
        copies.append(copy)
    total = part[at(chip), :]
    for d in range(1, chips):
        copies[d - 1].wait_recv()
        total = total + parts[d - 1]
    gram_ref[core, at(chip), :] = total
    results = []
    for d in range(1, 2 * chips):
        peer = lax.rem(me + d, 2 * chips)
        copy = pltpu.make_async_remote_copy(
            src_ref=gram_ref.at[core, at(chip)], dst_ref=gram_ref.at[core, at(chip)],
            send_sem=out_send.at[d - 1], recv_sem=out_recv.at[d - 1],
            device_id={"row": peer}, device_id_type=MESH,
        )
        copy.start()
        results.append(copy)
    for copy in copies:
        copy.wait_send()
    for copy in results:
        copy.wait()

    factor_body(scale, gram_ref, r_ref, own_w_ref, other_w_ref, work, roots)

    @pl.when(snap == 0)
    def _():
        for u in range(units):
            bulk(u).wait_send()

    @pl.when(snap == 1)
    def _():
        for u in range(halfway, units):
            bulk(u).wait_send()
        for u in range(halfway, units):
            bulk(u).wait_recv()


def exchange_and_factor(snapshots, counts, scale, units=32):
    narrow, slots = snapshots.shape
    dtype = snapshots.dtype
    n = lax.axis_size("row")
    chips = n // 2
    rows = narrow // 2
    height = 3 * rows
    f32 = jnp.float32
    vmem = pl.BlockSpec(memory_space=pltpu.VMEM)
    dma = pltpu.SemaphoreType.DMA
    return pl.pallas_call(
        functools.partial(panel_kernel, units, scale),
        name="exchange_and_factor",
        out_shape=(
            jax.ShapeDtypeStruct((narrow, slots), dtype),
            jax.ShapeDtypeStruct((narrow, slots), dtype),
            jax.ShapeDtypeStruct((2 * narrow, 2 * narrow), f32),
            jax.ShapeDtypeStruct((narrow, narrow), dtype),
            jax.ShapeDtypeStruct((narrow, narrow), dtype),
        ),
        in_specs=[
            pl.BlockSpec(memory_space=pltpu.SMEM),
            pl.BlockSpec(memory_space=pltpu.HBM),
        ],
        out_specs=(vmem, vmem, vmem, vmem, vmem),
        scratch_shapes=[
            pltpu.VMEM((2, narrow, narrow), f32),
            pltpu.VMEM((2, rows, narrow), f32),
            pltpu.VMEM((2, rows, narrow), f32),
            pltpu.VMEM((2, rows, narrow), f32),
            pltpu.VMEM((height, narrow), f32),
            pltpu.VMEM((chips - 1, height // chips, narrow), f32),
            pltpu.VMEM((2, height, narrow), f32),
            pltpu.VMEM((2, narrow, narrow), f32),
            pltpu.VMEM((narrow, narrow), f32),
            dma((8,)),
            dma((units,)),
            dma((units,)),
            pltpu.SemaphoreType.REGULAR((3,)),
            dma((2,)),
            dma((2,)),
            dma((2,)),
            dma((2,)),
            dma((chips - 1,)),
            dma((chips - 1,)),
            dma((n - 1,)),
            dma((n - 1,)),
            dma((1,)),
            dma((1,)),
        ],
        compiler_params=pltpu.CompilerParams(
            collective_id=0, has_side_effects=True, vmem_limit_bytes=44 << 20
        ),
    )(counts, snapshots)


def basis_kernel(pieces, counts_ref, own_w, other_w, r_in, own_ref, got_ref, out_ref, r_out, stage, sems):
    snap = lax.axis_index("snap")
    narrow, slots = own_ref.shape
    step = slots // pieces
    count = counts_ref[0]

    def piece(c):
        at = pl.ds(c * step, step)
        return pltpu.make_async_copy(stage.at[:, at], out_ref.at[:, at], sems.at[c])

    def form(weights, block, c):
        value = lax.dot_general(
            weights, block, (((1,), (0,)), ((), ())), preferred_element_type=jnp.float32
        )
        lane = lax.broadcasted_iota(jnp.int32, value.shape, 1) + c * step
        value = jnp.where(lane < count, value, 0.0).astype(stage.dtype)
        stage[:, c * step:(c + 1) * step] = value
        piece(c).start()

    @pl.when(snap == 0)
    def _():
        weights = own_w[...]
        for c in range(pieces):
            form(weights, own_ref[:, c * step:(c + 1) * step], c)

    @pl.when(snap == 1)
    def _():
        weights = jnp.concatenate([own_w[...], other_w[...]], axis=1)
        for c in range(pieces):
            here = slice(c * step, (c + 1) * step)
            form(weights, jnp.concatenate([own_ref[:, here], got_ref[:, here]], axis=0), c)

    r_out[...] = r_in[...]
    for c in range(pieces):
        piece(c).wait()


def form_basis(counts, own_w, other_w, r_factor, own, got, pieces=8):
    narrow, slots = own.shape
    vmem = pl.BlockSpec(memory_space=pltpu.VMEM)
    return pl.pallas_call(
        functools.partial(basis_kernel, pieces),
        name="form_basis",
        out_shape=(
            jax.ShapeDtypeStruct((narrow, slots), own.dtype),
            jax.ShapeDtypeStruct(r_factor.shape, r_factor.dtype),
        ),
        in_specs=[pl.BlockSpec(memory_space=pltpu.SMEM), vmem, vmem, vmem, vmem, vmem],
        out_specs=(pl.BlockSpec(memory_space=pltpu.HBM), vmem),
        scratch_shapes=[
            pltpu.VMEM((narrow, slots), own.dtype),
            pltpu.SemaphoreType.DMA((pieces,)),
        ],
        compiler_params=pltpu.CompilerParams(vmem_limit_bytes=16 << 20),
        cost_estimate=pl.CostEstimate(
            flops=4 * narrow * narrow * slots, bytes_accessed=8 * narrow * slots, transcendentals=0
        ),
    )(counts, own_w, other_w, r_factor, own, got)


def halves(snapshots, counts):
    slots = snapshots.shape[1]
    scale = math.sqrt(slots * lax.axis_size("row"))
    own, got, r_factor, own_w, other_w = exchange_and_factor(snapshots, counts, scale)
    return form_basis(counts, own_w, other_w, r_factor, own, got)


def two_halves(mesh):
    return mesh.shape["snap"] == 2 and mesh.shape["row"] == 16


def solution(mesh):
    placed = (P("snap", "row"), P("row"))
    body = halves if two_halves(mesh) else shards
    return jax.shard_map(
        body, mesh=mesh, in_specs=placed, out_specs=(P("snap", "row"), P()), check_vma=False
    )
```

time: 102 us -> 101 us (level)
  Pallas kernels: 85.7 us -> 98.6 us
  waiting for transfers between devices: 9.35 us -> 0 us
  starting transfers between devices: 2.98 us -> 0 us
    pallas_call x6 -> x2, Pallas kernels: 85.7 us -> 98.6 us  [the longest x1 95.5 us: exchange_and_factor(): pl.pallas_call(functools.partial(panel_kernel, units, scale), name='excha...]
    ppermute x2 -> x0, waiting for transfers between devices: 9.35 us -> none  [halves(): got[1:] = [lax.ppermute(piece, 'snap', [(0, 1)]) for piece in got[1:]]]
    ppermute x2 -> x0, starting transfers between devices: 2.98 us -> none  [halves(): got[1:] = [lax.ppermute(piece, 'snap', [(0, 1)]) for piece in got[1:]]]
  transfers between devices with their start and end apart: 2 -> 0, of which waited for: 2 -> 0; matrix products, arithmetic and copies ran while one was open for 0% -> 0% of each run, Pallas kernels for 30% -> 0%
where the time goes in v1:
time: 101 us; the launch traced here: 99.8 us
  Pallas kernels  98.6 us (98%)
  between operations  1.28 us (1%)
    pallas_call x1, Pallas kernels, exchange_and_factor(): pl.pallas_call(functools.partial(panel_kernel, units, scale), name='excha...  95.5 us
    pallas_call x1, Pallas kernels, form_basis(): pl.pallas_call(functools.partial(basis_kernel, pieces), name='form_basis'...  3.1 us

profile of v1, /device:TPU:31, one launch (start us, length us, event | category | flops | bytes accessed | tf_op | source)
XLA Modules:
  0.0 99.8 jit_solution(16003497142413942429)
XLA Ops:
  1.3 95.5 %exchange_and_factor.1 = (bf16[128,16384]{1,0:T(8,128)(2,1)S(1)}, bf16[128,16384]{1,0:T(8,128)(2,1)S(1)}, f32[256,256]{1,0:T(8,128)S(1)}, bf16[128,128]{1,0:T(8,128)(2,1)S(1)}, bf16[128,128]{1,0:T(8,128)(2,1)S(1)}) custom-call(s32[1]{0:T(128)S(6)} %copy.4.counts_ref, bf16[128,16384]{1,0:T(8,128)(2,1)} %x_ref.1), custom_call_target="tpu_custom_call" | custom-call | tf_op jit(solution)/shard_map/exchange_and_factor/pallas_call | solution.py:377
  96.7 3.1 %form_basis.1 = (bf16[128,16384]{1,0:T(8,128)(2,1)}, f32[256,256]{1,0:T(8,128)}) custom-call(s32[1]{0:T(128)S(6)} %copy.4.counts_ref, bf16[128,128]{1,0:T(8,128)(2,1)S(1)} %get-tuple-element.7.own_w, bf16[128,128]{1,0:T(8,128)(2,1)S(1)} %get-tuple-element.8.other_w, f32[256,256]{1,0:T(8,128)S(1)} %get-tuple-element.9.r_in, ...), custom_call_target="tpu_custom_call" | custom-call | flops 1073741824 | bytes 16777216 | tf_op jit(solution)/shard_map/form_basis/pallas_call | solution.py:463

commit v2 on v1

--- a/solution.py
+++ b/solution.py
@@ -178,21 +178,25 @@
 
 
 def panel_kernel(
-    units, scale, counts_ref, x_ref, own, got, r_ref, own_w_ref, other_w_ref,
+    units, mid, per, room, scale, counts_ref, x_ref,
+    own_low, own_top, got, top, r_ref, own_w_ref, other_w_ref, load_ref,
     mine, near, summed, theirs, part, parts, gram_ref, work, roots,
+    tally, tally_s, loose, packed, back,
     load_sem, send_sem, recv_sem, met, near_send, near_recv, sum_send, sum_recv,
-    part_send, part_recv, out_send, out_recv, pair_send, pair_recv,
+    part_send, part_recv, out_send, out_recv, tally_send, tally_recv, tally_copy,
+    loose_send, loose_recv, loose_copy, pack_send, pack_recv, back_send, back_recv,
 ):
     snap = lax.axis_index("snap")
     me = lax.axis_index("row")
+    n = lax.axis_size("row")
     core, chip = lax.rem(me, 2), lax.div(me, 2)
-    chips = lax.axis_size("row") // 2
+    chips = n // 2
     other = {"snap": 1 - snap}
     pair = {"row": me + 1 - 2 * core}
     narrow, slots = x_ref.shape
     step = slots // units
-    halfway = units // 2
-    half = slots // 2
+    base = got.shape[1]
+    low = base // step
     count = counts_ref[0]
     rows = narrow // 2
     y, z = lax.rem(chip, 2), lax.div(chip, 2)
@@ -215,61 +219,106 @@
     def _():
         greet({"row": me + 4})
 
+    tally[me] = jnp.full(tally.shape[1:], count, jnp.int32)
     wide = 8
     span = slots // wide
     loads = []
     for c in range(wide):
         at = pl.ds(c * span, span)
-        copy = pltpu.make_async_copy(x_ref.at[:, at], own.at[:, at], load_sem.at[c])
+        into, start = (own_low, c * span) if c * span < base else (own_top, c * span - base)
+        copy = pltpu.make_async_copy(
+            x_ref.at[:, at], into.at[:, pl.ds(start, span)], load_sem.at[c]
+        )
         copy.start()
         loads.append(copy)
 
     pl.semaphore_wait(barrier, 2 + meetings(chip))
 
     def bulk(u):
-        at = pl.ds(u * step, step)
+        into, start = (got, u * step) if u < low else (top, (u - low) * step)
         return pltpu.make_async_remote_copy(
-            src_ref=x_ref.at[:, at], dst_ref=got.at[:, at],
+            src_ref=x_ref.at[:, pl.ds(u * step, step)], dst_ref=into.at[:, pl.ds(start, step)],
             send_sem=send_sem.at[u], recv_sem=recv_sem.at[u],
             device_id=other, device_id_type=MESH,
         )
 
-    def send(low, high):
-        @pl.when(snap == 0)
+    def arrived(u):
+        if u < low:
+            return got[:, u * step:(u + 1) * step]
+        return top[:, (u - low) * step:(u - low + 1) * step]
+
+    def send(which, first, stop):
+        @pl.when(snap == which)
         def _():
-            for u in range(low, high):
+            for u in range(first, stop):
                 bulk(u).start()
 
-        top = min(high, halfway)
-
-        @pl.when(snap == 1)
-        def _():
-            for u in range(low, top):
-                bulk(halfway + u).start()
-
-    send(0, 6)
+    ahead = 6
+    behind = ahead + 5
+    send(0, 0, ahead)
+    send(1, mid, mid + ahead)
+
+    for stage in range(met.shape[0]):
+        meet(met, stage, chip, core)
+        pl.semaphore_wait(met.at[stage], meetings(chip))
+
+    def tally_to(d):
+        return pltpu.make_async_remote_copy(
+            src_ref=tally.at[me], dst_ref=tally.at[me],
+            send_sem=tally_send.at[d - 1], recv_sem=tally_recv.at[d - 1],
+            device_id={"row": lax.rem(me + d, n)}, device_id_type=MESH,
+        )
+
+    for d in range(1, n):
+        tally_to(d).start()
+
+    def loose_to(d, q):
+        at = (d - 1) * per + q
+        return pltpu.make_async_remote_copy(
+            src_ref=x_ref.at[:, pl.ds(base + LANES * (d + n * q), LANES)],
+            dst_ref=loose.at[me + n * q],
+            send_sem=loose_send.at[at], recv_sem=loose_recv.at[at],
+            device_id={"row": lax.rem(me + d, n)}, device_id_type=MESH,
+        )
+
+    def loose_own(q):
+        return pltpu.make_async_copy(
+            x_ref.at[:, pl.ds(base + LANES * n * q, LANES)], loose.at[me + n * q],
+            loose_copy.at[q],
+        )
+
+    hops = [(d, q) for q in range(per) for d in range(1, n)]
+
+    @pl.when(snap == 0)
+    def _():
+        for d, q in hops:
+            loose_to(d, q).start()
+        for q in range(per):
+            loose_own(q).start()
 
     def masked(block, start):
         lane = lax.broadcasted_iota(jnp.int32, block.shape, 1) + start
         return jnp.where(lane < count, block, jnp.zeros_like(block))
 
+    def owned(start, size):
+        if start < base:
+            return own_low[:, start:start + size]
+        return own_top[:, start - base:start - base + size]
+
     total = jnp.zeros((narrow, narrow), jnp.float32)
     for c in range(wide):
         loads[c].wait()
-        block = own[:, c * span:(c + 1) * span]
+        block = owned(c * span, span)
         total = total + mxu_nt(masked(block, c * span), block)
     mine[0] = total
 
-    def near_copy(i):
-        return pltpu.make_async_remote_copy(
+    def sum_copy(i):
+        away = pltpu.make_async_remote_copy(
             src_ref=mine.at[i, pl.ds(pl.multiple_of((1 - core) * rows, SUBLANES), rows)],
             dst_ref=near.at[i],
             send_sem=near_send.at[i], recv_sem=near_recv.at[i],
             device_id=pair, device_id_type=MESH,
         )
-
-    def sum_copy(i):
-        away = near_copy(i)
         away.start()
         away.wait()
         kept = mine[i, pl.ds(pl.multiple_of(core * rows, SUBLANES), rows), :]
@@ -282,31 +331,97 @@
 
     diagonal = sum_copy(0)
     diagonal.start()
-    send(6, halfway + 1)
-
-    for stage in range(met.shape[0]):
-        meet(met, stage, chip, core)
-        pl.semaphore_wait(met.at[stage], meetings(chip))
-
+    send(0, ahead, behind)
+    send(1, mid + ahead, units)
     mine[1] = jnp.zeros((narrow, narrow), jnp.float32)
-    for u in range(halfway):
-        @pl.when(snap == 1)
-        def _():
+
+    def cross(first, stop):
+        for u in range(first, stop):
             bulk(u).wait_recv()
-            start = u * step
-            block = masked(own[:, start:start + step], start)
-            mine[1] = mine[1] + mxu_nt(got[:, start:start + step], block)
-
-        @pl.when(snap == 0)
-        def _():
-            bulk(halfway + u).wait_recv()
-            start = half + u * step
-            block = masked(own[:, start:start + step], start)
-            mine[1] = mine[1] + mxu_nt(block, got[:, start:start + step])
+            block = masked(owned(u * step, step), u * step)
+
+            @pl.when(snap == 1)
+            def _():
+                mine[1] = mine[1] + mxu_nt(arrived(u), block)
+
+            @pl.when(snap == 0)
+            def _():
+                mine[1] = mine[1] + mxu_nt(block, arrived(u))
+
+    def learn():
+        for d in range(1, n):
+            tally_to(d).wait_recv()
+        copy = pltpu.make_async_copy(tally, tally_s, tally_copy)
+        copy.start()
+        copy.wait()
+        seen, before = jnp.int32(0), []
+        for q in range(per):
+            for i in range(n):
+                rel = lax.rem(me - i + n, n)
+                live = (base + LANES * (rel + n * q) < tally_s[i, 0, 0]).astype(jnp.int32)
+                before.append(seen)
+                seen = seen + live
+        return before, before[1:] + [seen]
+
+    def pack_to(h):
+        size = (room // 2, room - room // 2)[h]
+        at = pl.ds(h * (room // 2), size)
+        return pltpu.make_async_remote_copy(
+            src_ref=packed.at[0, at], dst_ref=packed.at[1, at],
+            send_sem=pack_send.at[h], recv_sem=pack_recv.at[h],
+            device_id=other, device_id_type=MESH,
+        )
+
+    def back_to(d, q):
+        at = (d - 1) * per + q
+        home = lax.rem(me + n - d, n)
+        return pltpu.make_async_remote_copy(
+            src_ref=back.at[home + n * q],
+            dst_ref=top.at[:, pl.ds(LANES * (d + n * q), LANES)],
+            send_sem=back_send.at[at], recv_sem=back_recv.at[at],
+            device_id={"row": home}, device_id_type=MESH,
+        )
+
+    @pl.when(snap == 0)
+    def _():
+        cross(mid, mid + 9)
+        _, after = learn()
+        for q in range(per):
+            loose_own(q).wait()
+        for d, q in hops:
+            loose_to(d, q).wait_recv()
+        for p in range(room):
+            pick = jnp.int32(0)
+            for passed in after:
+                pick = pick + (passed <= p).astype(jnp.int32)
+            pick = jnp.minimum(pick, per * n - 1)
+            packed[0, p] = loose[pick]
+        for h in range(2):
+            pack_to(h).start()
+        for u in range(behind, mid + 1):
+            bulk(u).start()
+        cross(mid + 9, units)
+
+    split = len(hops) // 2
+
+    @pl.when(snap == 1)
+    def _():
+        cross(0, behind)
+        before, _ = learn()
+        for h in range(2):
+            pack_to(h).wait_recv()
+        for f, place in enumerate(before):
+            place = jnp.minimum(place, room - 1)
+            back[f] = packed[1, place]
+        for d, q in hops[:split]:
+            back_to(d, q).start()
+        for q in range(per):
+            top[:, LANES * n * q:LANES * (n * q + 1)] = back[me + n * q]
+        cross(behind, mid)
 
     crossed = sum_copy(1)
     crossed.start()
-    send(halfway + 1, units)
+    send(0, mid + 1, low)
 
     diagonal.wait()
     part[0:rows, :] = jnp.where(snap == 0, summed[0], theirs[0])
@@ -335,8 +450,8 @@
         total = total + parts[d - 1]
     gram_ref[core, at(chip), :] = total
     results = []
-    for d in range(1, 2 * chips):
-        peer = lax.rem(me + d, 2 * chips)
+    for d in range(1, n):
+        peer = lax.rem(me + d, n)
         copy = pltpu.make_async_remote_copy(
             src_ref=gram_ref.at[core, at(chip)], dst_ref=gram_ref.at[core, at(chip)],
             send_sem=out_send.at[d - 1], recv_sem=out_recv.at[d - 1],
@@ -344,6 +459,12 @@
         )
         copy.start()
         results.append(copy)
+
+    @pl.when(snap == 1)
+    def _():
+        for d, q in hops[split:]:
+            back_to(d, q).start()
+
     for copy in copies:
         copy.wait_send()
     for copy in results:
@@ -351,44 +472,64 @@
 
     factor_body(scale, gram_ref, r_ref, own_w_ref, other_w_ref, work, roots)
 
+    lane = lax.broadcasted_iota(jnp.int32, tally.shape[1:], 1)
+    full = jnp.zeros(tally.shape[1:], jnp.int32)
+    for i in range(n):
+        rel = jnp.where(lane >= i, lane - i, lane - i + n)
+        for q in range(per):
+            full = full + jnp.where(base + LANES * (rel + n * q) < tally[i], 1, 0)
+    full = jnp.where(lane < n, full, 0).astype(jnp.float32)
+    load_ref[0, 0] = jnp.max(full)
+
+    for d in range(1, n):
+        tally_to(d).wait_send()
+
     @pl.when(snap == 0)
     def _():
-        for u in range(units):
+        for h in range(2):
+            pack_to(h).wait_send()
+        for d, q in hops:
+            loose_to(d, q).wait_send()
+        for u in range(low):
             bulk(u).wait_send()
 
     @pl.when(snap == 1)
     def _():
-        for u in range(halfway, units):
+        for u in range(mid, units):
             bulk(u).wait_send()
-        for u in range(halfway, units):
+        for d, q in hops:
+            back_to(d, q).wait()
+        for u in range(mid, low):
             bulk(u).wait_recv()
 
 
-def exchange_and_factor(snapshots, counts, scale, units=32):
+def exchange_and_factor(snapshots, counts, scale, room, per, units=32):
     narrow, slots = snapshots.shape
     dtype = snapshots.dtype
     n = lax.axis_size("row")
     chips = n // 2
     rows = narrow // 2
     height = 3 * rows
+    tail = per * n * LANES
     f32 = jnp.float32
     vmem = pl.BlockSpec(memory_space=pltpu.VMEM)
+    smem = pl.BlockSpec(memory_space=pltpu.SMEM)
     dma = pltpu.SemaphoreType.DMA
     return pl.pallas_call(
-        functools.partial(panel_kernel, units, scale),
+        functools.partial(panel_kernel, units, 14, per, room, scale),
         name="exchange_and_factor",
         out_shape=(
-            jax.ShapeDtypeStruct((narrow, slots), dtype),
-            jax.ShapeDtypeStruct((narrow, slots), dtype),
+            jax.ShapeDtypeStruct((narrow, slots - tail), dtype),
+            jax.ShapeDtypeStruct((narrow, tail), dtype),
+            jax.ShapeDtypeStruct((narrow, slots - tail), dtype),
+            jax.ShapeDtypeStruct((narrow, tail), dtype),
             jax.ShapeDtypeStruct((2 * narrow, 2 * narrow), f32),
             jax.ShapeDtypeStruct((narrow, narrow), dtype),
             jax.ShapeDtypeStruct((narrow, narrow), dtype),
+            jax.ShapeDtypeStruct((1, 1), f32),
         ),
-        in_specs=[
-            pl.BlockSpec(memory_space=pltpu.SMEM),
-            pl.BlockSpec(memory_space=pltpu.HBM),
-        ],
-        out_specs=(vmem, vmem, vmem, vmem, vmem),
+        in_specs=[smem, pl.BlockSpec(memory_space=pltpu.HBM)],
+        out_specs=(vmem, vmem, vmem, vmem, vmem, vmem, vmem, smem),
         scratch_shapes=[
             pltpu.VMEM((2, narrow, narrow), f32),
             pltpu.VMEM((2, rows, narrow), f32),
@@ -399,10 +540,15 @@
             pltpu.VMEM((2, height, narrow), f32),
             pltpu.VMEM((2, narrow, narrow), f32),
             pltpu.VMEM((narrow, narrow), f32),
+            pltpu.VMEM((n, 1, LANES), jnp.int32),
+            pltpu.SMEM((n, 1, LANES), jnp.int32),
+            pltpu.VMEM((per * n, narrow, LANES), dtype),
+            pltpu.VMEM((2, room, narrow, LANES), dtype),
+            pltpu.VMEM((per * n, narrow, LANES), dtype),
             dma((8,)),
             dma((units,)),
             dma((units,)),
-            pltpu.SemaphoreType.REGULAR((3,)),
+            pltpu.SemaphoreType.REGULAR((4,)),
             dma((2,)),
             dma((2,)),
             dma((2,)),
@@ -411,8 +557,16 @@
             dma((chips - 1,)),
             dma((n - 1,)),
             dma((n - 1,)),
-            dma((1,)),
-            dma((1,)),
+            dma((n - 1,)),
+            dma((n - 1,)),
+            dma,
+            dma((per * (n - 1),)),
+            dma((per * (n - 1),)),
+            dma((per,)),
+            dma((2,)),
+            dma((2,)),
+            dma((per * (n - 1),)),
+            dma((per * (n - 1),)),
         ],
         compiler_params=pltpu.CompilerParams(
             collective_id=0, has_side_effects=True, vmem_limit_bytes=44 << 20
@@ -420,21 +574,54 @@
     )(counts, snapshots)
 
 
-def basis_kernel(pieces, counts_ref, own_w, other_w, r_in, own_ref, got_ref, out_ref, r_out, stage, sems):
+def resend_kernel(x_ref, top_ref, send_sem, recv_sem):
     snap = lax.axis_index("snap")
-    narrow, slots = own_ref.shape
-    step = slots // pieces
+    other = {"snap": 1 - snap}
+    start = x_ref.shape[1] - top_ref.shape[1]
+    barrier = pltpu.get_barrier_semaphore()
+    pl.semaphore_signal(barrier, inc=1, device_id=other, device_id_type=MESH)
+    pl.semaphore_wait(barrier, 1)
+    copy = pltpu.make_async_remote_copy(
+        src_ref=x_ref.at[:, pl.ds(start, top_ref.shape[1])], dst_ref=top_ref,
+        send_sem=send_sem, recv_sem=recv_sem, device_id=other, device_id_type=MESH,
+    )
+    copy.start()
+    copy.wait()
+
+
+def resend(snapshots, tail):
+    return pl.pallas_call(
+        resend_kernel,
+        name="resend",
+        out_shape=jax.ShapeDtypeStruct((snapshots.shape[0], tail), snapshots.dtype),
+        in_specs=[pl.BlockSpec(memory_space=pl.ANY)],
+        out_specs=pl.BlockSpec(memory_space=pl.ANY),
+        scratch_shapes=[pltpu.SemaphoreType.DMA, pltpu.SemaphoreType.DMA],
+        compiler_params=pltpu.CompilerParams(collective_id=1, has_side_effects=True),
+    )(snapshots)
+
+
+def basis_kernel(first, pieces, counts_ref, own_w, other_w, own_ref, got_ref, *rest):
+    if first == 0:
+        r_in, load_in, out_ref, r_out, load_out, stage, sems = rest
+        load_out[0, 0] = load_in[0, 0]
+    else:
+        _, out_ref, stage, sems = rest
+    snap = lax.axis_index("snap")
+    step = own_ref.shape[1] // pieces
     count = counts_ref[0]
 
     def piece(c):
-        at = pl.ds(c * step, step)
-        return pltpu.make_async_copy(stage.at[:, at], out_ref.at[:, at], sems.at[c])
+        return pltpu.make_async_copy(
+            stage.at[:, pl.ds(c * step, step)], out_ref.at[:, pl.ds(first + c * step, step)],
+            sems.at[c],
+        )
 
     def form(weights, block, c):
         value = lax.dot_general(
             weights, block, (((1,), (0,)), ((), ())), preferred_element_type=jnp.float32
         )
-        lane = lax.broadcasted_iota(jnp.int32, value.shape, 1) + c * step
+        lane = lax.broadcasted_iota(jnp.int32, value.shape, 1) + first + c * step
         value = jnp.where(lane < count, value, 0.0).astype(stage.dtype)
         stage[:, c * step:(c + 1) * step] = value
         piece(c).start()
@@ -452,39 +639,57 @@
             here = slice(c * step, (c + 1) * step)
             form(weights, jnp.concatenate([own_ref[:, here], got_ref[:, here]], axis=0), c)
 
-    r_out[...] = r_in[...]
+    if first == 0:
+        r_out[...] = r_in[...]
     for c in range(pieces):
         piece(c).wait()
 
 
-def form_basis(counts, own_w, other_w, r_factor, own, got, pieces=8):
-    narrow, slots = own.shape
+def form_basis(counts, own_w, other_w, own, got, first, slots, *more, step=2048):
+    narrow, width = own.shape
+    pieces = width // step
     vmem = pl.BlockSpec(memory_space=pltpu.VMEM)
+    smem = pl.BlockSpec(memory_space=pltpu.SMEM)
+    hbm = pl.BlockSpec(memory_space=pltpu.HBM)
+    out_shape = [jax.ShapeDtypeStruct((narrow, slots), own.dtype)]
+    out_specs = [hbm]
+    if first == 0:
+        out_shape += [jax.ShapeDtypeStruct(m.shape, m.dtype) for m in more]
+        out_specs += [vmem, smem]
+        more_specs = [vmem, smem]
+    else:
+        more_specs = [hbm]
     return pl.pallas_call(
-        functools.partial(basis_kernel, pieces),
+        functools.partial(basis_kernel, first, pieces),
         name="form_basis",
-        out_shape=(
-            jax.ShapeDtypeStruct((narrow, slots), own.dtype),
-            jax.ShapeDtypeStruct(r_factor.shape, r_factor.dtype),
-        ),
-        in_specs=[pl.BlockSpec(memory_space=pltpu.SMEM), vmem, vmem, vmem, vmem, vmem],
-        out_specs=(pl.BlockSpec(memory_space=pltpu.HBM), vmem),
+        out_shape=out_shape,
+        in_specs=[smem, vmem, vmem, vmem, vmem, *more_specs],
+        out_specs=out_specs,
+        input_output_aliases={5: 0} if first else {},
         scratch_shapes=[
-            pltpu.VMEM((narrow, slots), own.dtype),
+            pltpu.VMEM((narrow, width), own.dtype),
             pltpu.SemaphoreType.DMA((pieces,)),
         ],
         compiler_params=pltpu.CompilerParams(vmem_limit_bytes=16 << 20),
         cost_estimate=pl.CostEstimate(
-            flops=4 * narrow * narrow * slots, bytes_accessed=8 * narrow * slots, transcendentals=0
+            flops=4 * narrow * narrow * width, bytes_accessed=8 * narrow * width, transcendentals=0
         ),
-    )(counts, own_w, other_w, r_factor, own, got)
-
-
-def halves(snapshots, counts):
+    )(counts, own_w, other_w, own, got, *more)
+
+
+def halves(snapshots, counts, room=17, per=2):
     slots = snapshots.shape[1]
     scale = math.sqrt(slots * lax.axis_size("row"))
-    own, got, r_factor, own_w, other_w = exchange_and_factor(snapshots, counts, scale)
-    return form_basis(counts, own_w, other_w, r_factor, own, got)
+    own, own_top, got, top, r_factor, own_w, other_w, load = exchange_and_factor(
+        snapshots, counts, scale, room, per
+    )
+    form = functools.partial(form_basis, counts, own_w, other_w)
+    basis, r_factor, load = form(own, got, 0, slots, r_factor, load)
+    top = lax.cond(
+        load[0, 0] > room, lambda kept: resend(snapshots, kept.shape[1]), lambda kept: kept, top
+    )
+    (basis,) = form(own_top, top, own.shape[1], slots, basis)
+    return (basis, r_factor)
 
 
 def two_halves(mesh):

time: 101 us -> 97.4 us (0.964)
  Pallas kernels: 98.6 us -> 95.1 us
    pallas_call x2 -> x3, Pallas kernels: 98.6 us -> 95.1 us  [the longest x1 90.4 us: exchange_and_factor(): pl.pallas_call(functools.partial(panel_kernel, units, 14, per, room, scal...]
where the time goes in v2:
time: 97.4 us; the launch traced here: 97.2 us
  Pallas kernels  95.1 us (98%)
  between operations  2.07 us (2%)
    pallas_call x1, Pallas kernels, exchange_and_factor(): pl.pallas_call(functools.partial(panel_kernel, units, 14, per, room, scal...  90.4 us
    pallas_call x2, Pallas kernels, form_basis(): pl.pallas_call(functools.partial(basis_kernel, first, pieces), name='form...  4.7 us

profile of v2, /device:TPU:31, one launch (start us, length us, event | category | flops | bytes accessed | tf_op | source)
XLA Modules:
  0.0 97.2 jit_solution(3989678977423600299)
XLA Ops:
  1.3 90.4 %exchange_and_factor.1 = (bf16[128,12288]{1,0:T(8,128)(2,1)S(1)}, bf16[128,4096]{1,0:T(8,128)(2,1)S(1)}, bf16[128,12288]{1,0:T(8,128)(2,1)S(1)}, bf16[128,4096]{...) custom-call(s32[1]{0:T(128)S(6)} %copy.8.counts_ref, ...), custom_call_target="tpu_custom_call" | custom-call | tf_op jit(solution)/shard_map/exchange_and_factor/pallas_call | solution.py:518
  91.7 3.4 %form_basis.2 = (bf16[128,16384]{1,0:T(8,128)(2,1)}, f32[256,256]{1,0:T(8,128)}, f32[1,1]{1,0:T(1,128)}) custom-call(s32[1]{0:T(128)S(6)} %copy.8.counts_ref, bf16[128,128]{1,0:T(8,128)(2,1)S(1)} %get-tuple-element.18.own_w, bf16[128,128]{1,0:T(8,128)(2,1)S(1)} %get-tuple-element.19.other_w, bf16[128,12288]{1,0:T(8,128)(2,1)S(1)} %get-tuple-element.21.own_ref, ...), custom_call_target="tpu_custom_call" | custom-call | flops 805306368 | bytes 12582912 | tf_op jit(solution)/shard_map/form_basis/pallas_call | solution.py:662
  95.7 1.3 %form_basis.3 = bf16[128,16384]{1,0:T(8,128)(2,1)} custom-call(s32[1]{0:T(128)S(6)} %copy.8.counts_ref, bf16[128,128]{1,0:T(8,128)(2,1)S(1)} %get-tuple-element.18.own_w, bf16[128,128]{1,0:T(8,128)(2,1)S(1)} %get-tuple-element.19.other_w, bf16[128,4096]{1,0:T(8,128)(2,1)S(1)} %get-tuple-element.20.own_ref, ...), custom_call_target="tpu_custom_call", output_to_operand_aliasing={{}: (5, {})} | custom-call | flops 268435456 | bytes 4194304 | tf_op jit(solution)/shard_map/form_basis/pallas_call | solution.py:662
  (1 shorter events, 0.0 us)

commit v3 on v2

--- a/solution.py
+++ b/solution.py
@@ -363,6 +363,16 @@
                 seen = seen + live
         return before, before[1:] + [seen]
 
+    def note_load():
+        lane = lax.broadcasted_iota(jnp.int32, tally.shape[1:], 1)
+        full = jnp.zeros(tally.shape[1:], jnp.int32)
+        for i in range(n):
+            rel = jnp.where(lane >= i, lane - i, lane - i + n)
+            for q in range(per):
+                full = full + jnp.where(base + LANES * (rel + n * q) < tally[i], 1, 0)
+        full = jnp.where(lane < n, full, 0).astype(jnp.float32)
+        load_ref[0, 0] = jnp.max(full)
+
     def pack_to(h):
         size = (room // 2, room - room // 2)[h]
         at = pl.ds(h * (room // 2), size)
@@ -400,14 +410,16 @@
             pack_to(h).start()
         for u in range(behind, mid + 1):
             bulk(u).start()
+        note_load()
         cross(mid + 9, units)
 
     split = len(hops) // 2
 
     @pl.when(snap == 1)
     def _():
-        cross(0, behind)
+        cross(0, 8)
         before, _ = learn()
+        cross(8, behind)
         for h in range(2):
             pack_to(h).wait_recv()
         for f, place in enumerate(before):
@@ -417,6 +429,7 @@
             back_to(d, q).start()
         for q in range(per):
             top[:, LANES * n * q:LANES * (n * q + 1)] = back[me + n * q]
+        note_load()
         cross(behind, mid)
 
     crossed = sum_copy(1)
@@ -460,26 +473,17 @@
         copy.start()
         results.append(copy)
 
-    @pl.when(snap == 1)
-    def _():
-        for d, q in hops[split:]:
-            back_to(d, q).start()
-
     for copy in copies:
         copy.wait_send()
     for copy in results:
         copy.wait()
 
+    @pl.when(snap == 1)
+    def _():
+        for d, q in hops[split:]:
+            back_to(d, q).start()
+
     factor_body(scale, gram_ref, r_ref, own_w_ref, other_w_ref, work, roots)
-
-    lane = lax.broadcasted_iota(jnp.int32, tally.shape[1:], 1)
-    full = jnp.zeros(tally.shape[1:], jnp.int32)
-    for i in range(n):
-        rel = jnp.where(lane >= i, lane - i, lane - i + n)
-        for q in range(per):
-            full = full + jnp.where(base + LANES * (rel + n * q) < tally[i], 1, 0)
-    full = jnp.where(lane < n, full, 0).astype(jnp.float32)
-    load_ref[0, 0] = jnp.max(full)
 
     for d in range(1, n):
         tally_to(d).wait_send()

time: 97.4 us -> 94.3 us (0.968)
  Pallas kernels: 95.1 us -> 91.2 us
    pallas_call x1, Pallas kernels: 90.4 us -> 86.5 us  [exchange_and_factor(): pl.pallas_call(functools.partial(panel_kernel, units, 14, per, room, scal...]
where the time goes in v3:
time: 94.3 us; the launch traced here: 93.3 us
  Pallas kernels  91.2 us (97%)
  between operations  2.07 us (2%)
    pallas_call x1, Pallas kernels, exchange_and_factor(): pl.pallas_call(functools.partial(panel_kernel, units, 14, per, room, scal...  86.5 us
    pallas_call x2, Pallas kernels, form_basis(): pl.pallas_call(functools.partial(basis_kernel, first, pieces), name='form...  4.69 us

profile of v3, /device:TPU:31, one launch (start us, length us, event | category | flops | bytes accessed | tf_op | source)
XLA Modules:
  0.0 93.3 jit_solution(5139435531114424822)
XLA Ops:
  1.3 86.5 %exchange_and_factor.1 = (bf16[128,12288]{1,0:T(8,128)(2,1)S(1)}, bf16[128,4096]{1,0:T(8,128)(2,1)S(1)}, bf16[128,12288]{1,0:T(8,128)(2,1)S(1)}, bf16[128,4096]{...) custom-call(s32[1]{0:T(128)S(6)} %copy.8.counts_ref, ...), custom_call_target="tpu_custom_call" | custom-call | tf_op jit(solution)/shard_map/exchange_and_factor/pallas_call | solution.py:522
  87.8 3.4 %form_basis.2 = (bf16[128,16384]{1,0:T(8,128)(2,1)}, f32[256,256]{1,0:T(8,128)}, f32[1,1]{1,0:T(1,128)}) custom-call(s32[1]{0:T(128)S(6)} %copy.8.counts_ref, bf16[128,128]{1,0:T(8,128)(2,1)S(1)} %get-tuple-element.18.own_w, bf16[128,128]{1,0:T(8,128)(2,1)S(1)} %get-tuple-element.19.other_w, bf16[128,12288]{1,0:T(8,128)(2,1)S(1)} %get-tuple-element.21.own_ref, ...), custom_call_target="tpu_custom_call" | custom-call | flops 805306368 | bytes 12582912 | tf_op jit(solution)/shard_map/form_basis/pallas_call | solution.py:666
  91.8 1.3 %form_basis.3 = bf16[128,16384]{1,0:T(8,128)(2,1)} custom-call(s32[1]{0:T(128)S(6)} %copy.8.counts_ref, bf16[128,128]{1,0:T(8,128)(2,1)S(1)} %get-tuple-element.18.own_w, bf16[128,128]{1,0:T(8,128)(2,1)S(1)} %get-tuple-element.19.other_w, bf16[128,4096]{1,0:T(8,128)(2,1)S(1)} %get-tuple-element.20.own_ref, ...), custom_call_target="tpu_custom_call", output_to_operand_aliasing={{}: (5, {})} | custom-call | flops 268435456 | bytes 4194304 | tf_op jit(solution)/shard_map/form_basis/pallas_call | solution.py:666
  (1 shorter events, 0.0 us)

commit v4 on v3

--- a/solution.py
+++ b/solution.py
@@ -607,8 +607,7 @@
 
 def basis_kernel(first, pieces, counts_ref, own_w, other_w, own_ref, got_ref, *rest):
     if first == 0:
-        r_in, load_in, out_ref, r_out, load_out, stage, sems = rest
-        load_out[0, 0] = load_in[0, 0]
+        r_in, out_ref, r_out, stage, sems = rest
     else:
         _, out_ref, stage, sems = rest
     snap = lax.axis_index("snap")
@@ -659,8 +658,8 @@
     out_specs = [hbm]
     if first == 0:
         out_shape += [jax.ShapeDtypeStruct(m.shape, m.dtype) for m in more]
-        out_specs += [vmem, smem]
-        more_specs = [vmem, smem]
+        out_specs += [vmem]
+        more_specs = [vmem]
     else:
         more_specs = [hbm]
     return pl.pallas_call(
@@ -688,7 +687,8 @@
         snapshots, counts, scale, room, per
     )
     form = functools.partial(form_basis, counts, own_w, other_w)
-    basis, r_factor, load = form(own, got, 0, slots, r_factor, load)
+    basis, r_factor = form(own, got, 0, slots, r_factor)
+    basis, load = lax.optimization_barrier((basis, load))
     top = lax.cond(
         load[0, 0] > room, lambda kept: resend(snapshots, kept.shape[1]), lambda kept: kept, top
     )

time: 94.3 us -> 93.7 us (level)
  no operation moved by 1% of the time
where the time goes in v4:
time: 93.7 us; the launch traced here: 92.7 us
  Pallas kernels  90.6 us (97%)
  between operations  2.09 us (2%)
    pallas_call x1, Pallas kernels, exchange_and_factor(): pl.pallas_call(functools.partial(panel_kernel, units, 14, per, room, scal...  86.5 us
    pallas_call x2, Pallas kernels, form_basis(): pl.pallas_call(functools.partial(basis_kernel, first, pieces), name='form...  4.07 us

profile of v4, /device:TPU:31, one launch (start us, length us, event | category | flops | bytes accessed | tf_op | source)
XLA Modules:
  0.0 92.7 jit_solution(7284990664950064689)
XLA Ops:
  1.3 86.5 %exchange_and_factor.1 = (bf16[128,12288]{1,0:T(8,128)(2,1)S(1)}, bf16[128,4096]{1,0:T(8,128)(2,1)S(1)}, bf16[128,12288]{1,0:T(8,128)(2,1)S(1)}, bf16[128,4096]{...) custom-call(s32[1]{0:T(128)S(6)} %copy.8.counts_ref, ...), custom_call_target="tpu_custom_call" | custom-call | tf_op jit(solution)/shard_map/exchange_and_factor/pallas_call | solution.py:522
  87.8 2.7 %form_basis.2 = (bf16[128,16384]{1,0:T(8,128)(2,1)}, f32[256,256]{1,0:T(8,128)}) custom-call(s32[1]{0:T(128)S(6)} %copy.8.counts_ref, bf16[128,128]{1,0:T(8,128)(2,1)S(1)} %get-tuple-element.19.own_w, bf16[128,128]{1,0:T(8,128)(2,1)S(1)} %get-tuple-element.20.other_w, bf16[128,12288]{1,0:T(8,128)(2,1)S(1)} %get-tuple-element.22.own_ref, ...), custom_call_target="tpu_custom_call" | custom-call | flops 805306368 | bytes 12582912 | tf_op jit(solution)/shard_map/form_basis/pallas_call | solution.py:665
  91.2 1.3 %form_basis.3 = bf16[128,16384]{1,0:T(8,128)(2,1)} custom-call(s32[1]{0:T(128)S(6)} %copy.8.counts_ref, bf16[128,128]{1,0:T(8,128)(2,1)S(1)} %get-tuple-element.19.own_w, bf16[128,128]{1,0:T(8,128)(2,1)S(1)} %get-tuple-element.20.other_w, bf16[128,4096]{1,0:T(8,128)(2,1)S(1)} %get-tuple-element.21.own_ref, ...), custom_call_target="tpu_custom_call", output_to_operand_aliasing={{}: (5, {})} | custom-call | flops 268435456 | bytes 4194304 | tf_op jit(solution)/shard_map/form_basis/pallas_call | solution.py:665
  (1 shorter events, 0.0 us)
